TPU v7x, 512 devices: a whole 4x4x16 slice. The times are simulated.
512 devices in a mesh: ctx: 128 (over y, z, core), head: 4 (over x).
Axes of the slice: x: 4, y: 4, z: 16, core: 2. Of those that a mesh axis runs over, the one named last changes fastest.
Arguments:
- branch_q: bfloat16 [16384, 4, 1024], P('ctx', 'head'), may hold values from -6 to 6
- branch_k: bfloat16 [16384, 4, 128], P('ctx', 'head'), may hold values from -6 to 6
- branch_v: bfloat16 [16384, 4, 128], P('ctx', 'head'), may hold values from -6 to 6
- branch_o: bfloat16 [16384, 4, 1024], P('ctx', 'head'), may hold values from -4 to 4
- branch_dout: bfloat16 [16384, 4, 1024], P('ctx', 'head'), may hold values from -512 to 512
- prompt_q: bfloat16 [256, 4, 1024], P('ctx', 'head'), may hold values from -6 to 6
- prompt_k: bfloat16 [256, 4, 128], P('ctx', 'head'), may hold values from -6 to 6
- prompt_v: bfloat16 [256, 4, 128], P('ctx', 'head'), may hold values from -6 to 6
- prompt_o: bfloat16 [256, 4, 1024], P('ctx', 'head'), may hold values from -4 to 4
- prompt_dout: bfloat16 [256, 4, 1024], P('ctx', 'head'), may hold values from -512 to 512
- gains: float32 [2, 128], replicated, may hold values from 0.8 to 2
- parents: int32 [128], P('ctx'), may hold values from 0 to 128, as said below
- depth: int32 [16384], P('ctx'), may hold values from 128 to 1279, as said below
Outputs:
- branch_dq: bfloat16 [16384, 4, 1024], P('ctx', 'head')
- branch_dk: bfloat16 [16384, 4, 128], P('ctx', 'head')
- branch_dv: bfloat16 [16384, 4, 128], P('ctx', 'head')
- prompt_dq: bfloat16 [256, 4, 1024], P('ctx', 'head')
- prompt_dk: bfloat16 [256, 4, 128], P('ctx', 'head')
- prompt_dv: bfloat16 [256, 4, 128], P('ctx', 'head')
- gain_grads: float32 [2, 128], replicated
Inputs may be any that keep to these rules, and one draw needn't show every extreme that they name: `parents`: the parent of a branch block is a prompt block or an earlier branch block of the same subtree. A subtree is a run of consecutive branch blocks whose first block's parent is a prompt block; a run has at most 8 blocks, and some run has exactly 8. depth of a branch token = 128 times the number of its block's proper ancestor blocks, prompt blocks up to the fork included, plus its offset in its block.
All inputs are finite; a program needn't handle non-finite values.
Results may differ from a plain program's by a relative error of at most 0.0093.
Values may be sent and summed in bfloat16 or wider, within the bound.
A program may use at most 64 MiB of HBM per device.

v0:
```python
import jax
import jax.numpy as jnp
from jax import lax
from jax.sharding import PartitionSpec as P

BLK = 128
SUB = 8
PFX = 256
EPS = 1e-06
THETA = 1000000.0


def shifted(value, axis, steps):
    count = lax.axis_size(axis)
    leading, last = (max(0, -steps), min(count, count - steps))
    return lax.ppermute(value, axis, [(source, source + steps) for source in range(leading, last)])


def angles(positions, head_size):
    half_size = head_size // 2
    frequencies = THETA ** (-(jnp.arange(half_size, dtype=jnp.float32) * 2.0) / head_size)
    return positions.astype(jnp.float32)[:, None] * frequencies[None, :]


def rotate(values, angle_table):
    half_size = values.shape[-1] // 2
    cosine = jnp.cos(angle_table)
    sine_part = jnp.sin(angle_table)
    first_half = values[..., :half_size]
    second_half = values[..., half_size:]
    return jnp.concatenate(
        [
            first_half * cosine - second_half * sine_part,
            second_half * cosine + first_half * sine_part,
        ],
        axis=-1,
    )


def prepare(raw_values, gain_vector, angle_table):
    widened = raw_values.astype(jnp.float32)
    inverse = lax.rsqrt(jnp.mean(widened * widened, axis=-1, keepdims=True) + EPS)
    unit_values = widened * inverse
    rotated = rotate(unit_values * gain_vector, angle_table).astype(jnp.bfloat16)
    return (unit_values, inverse, rotated)


def norm_back(grad_rotated, unit_values, inverse, gain_vector, angle_table):
    grad_normed = rotate(grad_rotated, -angle_table)
    scaled = grad_normed * gain_vector
    grad_raw = (
        scaled - unit_values * jnp.mean(scaled * unit_values, axis=-1, keepdims=True)
    ) * inverse
    gain_part = jnp.sum((grad_normed * unit_values).reshape(-1, unit_values.shape[-1]), axis=0)
    return (grad_raw, gain_part)


def per_device(
    branch_q,
    branch_k,
    branch_v,
    branch_o,
    branch_dout,
    prompt_q,
    prompt_k,
    prompt_v,
    prompt_o,
    prompt_dout,
    gains,
    parents,
    depth,
):
    head_size = branch_k.shape[-1]
    tok_local = branch_k.shape[0]
    prompt_local = prompt_k.shape[0]
    group_size = branch_q.shape[-1] // head_size
    blocks_local = tok_local // BLK
    reach_back = (SUB + blocks_local - 2) // blocks_local
    prompt_blocks = PFX // BLK
    piece_size = 2 * BLK
    score_scale = head_size ** (-0.5)
    device = lax.axis_index("ctx")
    gain_q = gains[0]
    gain_k = gains[1]
    row_count = tok_local + prompt_local
    angle_branch = angles(depth, head_size)
    angle_prompt = angles(
        device * prompt_local + jnp.arange(prompt_local, dtype=jnp.int32), head_size
    )
    angle_rows = jnp.concatenate([angle_branch, angle_prompt])[:, None, :]
    queries = jnp.concatenate([branch_q[:, 0], prompt_q[:, 0]]).reshape(
        row_count, group_size, head_size
    )
    unit_q, inverse_q, rotated_q = prepare(queries, gain_q, angle_rows)
    unit_bk, inverse_bk, rotated_bk = prepare(branch_k[:, 0], gain_k, angle_branch)
    unit_pk, inverse_pk, rotated_pk = prepare(prompt_k[:, 0], gain_k, angle_prompt)
    value_local = branch_v[:, 0]
    prompt_keys, prompt_values = (
        lax.all_gather(rotated_pk, "ctx", axis=0, tiled=True),
        lax.all_gather(prompt_v[:, 0], "ctx", axis=0, tiled=True),
    )
    fetched = [(rotated_bk, value_local, parents)]
    for distance in range(1, reach_back + 1):
        fetched.insert(0, shifted((rotated_bk, value_local, parents), "ctx", distance))
    window_k = jnp.stack([member[0] for member in fetched])
    window_v = jnp.stack([member[1] for member in fetched])
    window_parents = jnp.stack([member[2] for member in fetched])
    window_blocks = (reach_back + 1) * blocks_local
    flat_parents = window_parents.reshape(window_blocks)
    first_block = (device - reach_back) * blocks_local
    slot_ids = jnp.arange(window_blocks, dtype=jnp.int32)

    def climb(step_index, climb_state):
        current, ancestors, fork_blocks = climb_state
        branchy = current >= prompt_blocks
        located = current - prompt_blocks - first_block
        matched = (slot_ids[None, :] == located[:, None]) & branchy[:, None]
        upward = jnp.sum(jnp.where(matched, flat_parents[None, :], 0), axis=1).astype(jnp.int32)
        return (
            jnp.where(branchy, upward, current),
            ancestors | matched,
            jnp.where(branchy, fork_blocks, current),
        )

    start_state = (
        device * blocks_local + jnp.arange(blocks_local, dtype=jnp.int32) + prompt_blocks,
        jnp.zeros((blocks_local, window_blocks), dtype=bool),
        jnp.zeros((blocks_local,), jnp.int32),
    )
    unused, ancestors, fork_blocks = lax.fori_loop(0, SUB + 1, climb, start_state)
    offsets = jnp.arange(BLK, dtype=jnp.int32)
    branch_limit = jnp.broadcast_to(
        (BLK * (fork_blocks + 1))[:, None], (blocks_local, BLK)
    ).reshape(tok_local)
    prompt_limit = device * prompt_local + jnp.arange(prompt_local, dtype=jnp.int32) + 1
    row_limit = jnp.concatenate([branch_limit, prompt_limit])
    branch_seen = jnp.broadcast_to(
        ancestors[:, None, :], (blocks_local, BLK, window_blocks)
    ).reshape(tok_local, window_blocks)
    row_seen = jnp.concatenate([branch_seen, jnp.zeros((prompt_local, window_blocks), dtype=bool)])
    branch_own = jnp.broadcast_to(
        (reach_back * blocks_local + jnp.arange(blocks_local, dtype=jnp.int32))[:, None],
        (blocks_local, BLK),
    ).reshape(tok_local)
    row_own = jnp.concatenate([branch_own, jnp.full((prompt_local,), -1, jnp.int32)])
    row_offset = jnp.concatenate(
        [jnp.tile(offsets, blocks_local), jnp.zeros((prompt_local,), jnp.int32)]
    )

    def piece_mask(key_start):
        key_ids = key_start + jnp.arange(piece_size, dtype=jnp.int32)
        prompt_key = key_ids < PFX
        window_pos = key_ids - PFX
        key_block = window_pos // BLK
        key_offset = window_pos % BLK
        prompt_ok = prompt_key[None, :] & (key_ids[None, :] < row_limit[:, None])
        block_seen = jnp.any(
            row_seen[:, :, None] & (key_block[None, None, :] == slot_ids[None, :, None]), axis=1
        )
        causal = (key_block[None, :] != row_own[:, None]) | (
            key_offset[None, :] <= row_offset[:, None]
        )
        return prompt_ok | jnp.logical_not(prompt_key)[None, :] & block_seen & causal

    key_total = PFX + window_blocks * BLK
    piece_count = key_total // piece_size
    all_keys = jnp.concatenate([prompt_keys, window_k.reshape(-1, head_size)]).reshape(
        piece_count, piece_size, head_size
    )
    all_values = jnp.concatenate([prompt_values, window_v.reshape(-1, head_size)]).reshape(
        piece_count, piece_size, head_size
    )
    key_starts = jnp.arange(piece_count, dtype=jnp.int32) * piece_size
    query_rows = rotated_q.reshape(row_count * group_size, head_size)
    grad_rows = jnp.concatenate([branch_dout[:, 0], prompt_dout[:, 0]]).reshape(
        row_count * group_size, head_size
    )
    out_rows = jnp.concatenate([branch_o[:, 0], prompt_o[:, 0]]).reshape(
        row_count * group_size, head_size
    )
    row_delta = jnp.sum(
        grad_rows.astype(jnp.float32) * out_rows.astype(jnp.float32), axis=-1
    ).reshape(row_count, group_size)

    def scores_of(key_piece):
        products = jnp.einsum(
            "qd,kd->qk", query_rows, key_piece, preferred_element_type=jnp.float32
        )
        return products.reshape(row_count, group_size, piece_size) * score_scale

    def add_total(running, scan_item):
        key_start, key_piece = scan_item
        visible = piece_mask(key_start)[:, None, :]
        return (
            running + jnp.sum(jnp.where(visible, jnp.exp(scores_of(key_piece)), 0.0), axis=-1),
            None,
        )

    totals, unused_rows = lax.scan(
        add_total, jnp.zeros((row_count, group_size), jnp.float32), (key_starts, all_keys)
    )
    log_total = jnp.log(totals)

    def back_piece(grad_q, scan_item):
        key_start, key_piece, value_piece = scan_item
        visible = piece_mask(key_start)[:, None, :]
        weights = jnp.where(visible, jnp.exp(scores_of(key_piece) - log_total[:, :, None]), 0.0)
        weight_half = weights.astype(jnp.bfloat16).reshape(row_count * group_size, piece_size)
        grad_v = jnp.einsum("qk,qd->kd", weight_half, grad_rows, preferred_element_type=jnp.float32)
        grad_p = jnp.einsum(
            "qd,kd->qk", grad_rows, value_piece, preferred_element_type=jnp.float32
        ).reshape(row_count, group_size, piece_size)
        grad_s = (
            (weights * (grad_p - row_delta[:, :, None]))
            .astype(jnp.bfloat16)
            .reshape(row_count * group_size, piece_size)
        )
        grad_k = (
            jnp.einsum("qk,qd->kd", grad_s, query_rows, preferred_element_type=jnp.float32)
            * score_scale
        )
        added = grad_q + jnp.einsum(
            "qk,kd->qd", grad_s, key_piece, preferred_element_type=jnp.float32
        )
        return (added, (grad_k, grad_v))

    grad_q, piece_grads = lax.scan(
        back_piece,
        jnp.zeros((row_count * group_size, head_size), jnp.float32),
        (key_starts, all_keys, all_values),
    )
    grad_keys = piece_grads[0].reshape(key_total, head_size)
    grad_values = piece_grads[1].reshape(key_total, head_size)
    prompt_gk, prompt_gv = (
        lax.psum_scatter(grad_keys[:PFX], "ctx", scatter_dimension=0, tiled=True),
        lax.psum_scatter(grad_values[:PFX], "ctx", scatter_dimension=0, tiled=True),
    )
    window_gk = grad_keys[PFX:].reshape(reach_back + 1, tok_local, head_size)
    window_gv = grad_values[PFX:].reshape(reach_back + 1, tok_local, head_size)
    total_k = window_gk[reach_back]
    total_v = window_gv[reach_back]
    for distance in range(1, reach_back + 1):
        back_k, back_v = (
            shifted(window_gk[reach_back - distance].astype(jnp.bfloat16), "ctx", -distance).astype(
                jnp.float32
            ),
            shifted(window_gv[reach_back - distance].astype(jnp.bfloat16), "ctx", -distance).astype(
                jnp.float32
            ),
        )
        total_k = total_k + back_k
        total_v = total_v + back_v
    grad_all_q = (grad_q * score_scale).reshape(row_count, group_size, head_size)
    raw_q, gain_part_q = norm_back(grad_all_q, unit_q, inverse_q, gain_q, angle_rows)
    raw_bk, gain_bk = norm_back(total_k, unit_bk, inverse_bk, gain_k, angle_branch)
    raw_pk, gain_pk = norm_back(prompt_gk, unit_pk, inverse_pk, gain_k, angle_prompt)
    sum_q, sum_k = lax.psum((gain_part_q, gain_bk + gain_pk), ("ctx", "head"))
    token_total = (tok_local + prompt_local) * lax.axis_size("ctx")
    head_total = lax.axis_size("head")
    factor_q = (token_total * head_total * group_size) ** (-0.5)
    factor_k = (token_total * head_total) ** (-0.5)
    gain_grads = jnp.stack([sum_q * factor_q, sum_k * factor_k])
    branch_dq = raw_q[:tok_local].reshape(tok_local, 1, group_size * head_size).astype(jnp.bfloat16)
    prompt_dq = (
        raw_q[tok_local:].reshape(prompt_local, 1, group_size * head_size).astype(jnp.bfloat16)
    )
    return (
        branch_dq,
        raw_bk[:, None].astype(jnp.bfloat16),
        total_v[:, None].astype(jnp.bfloat16),
        prompt_dq,
        raw_pk[:, None].astype(jnp.bfloat16),
        prompt_gv[:, None].astype(jnp.bfloat16),
        gain_grads,
    )


def solution(mesh):
    return jax.shard_map(
        per_device,
        mesh=mesh,
        in_specs=(
            P("ctx", "head", None),
            P("ctx", "head", None),
            P("ctx", "head", None),
            P("ctx", "head", None),
            P("ctx", "head", None),
            P("ctx", "head", None),
            P("ctx", "head", None),
            P("ctx", "head", None),
            P("ctx", "head", None),
            P("ctx", "head", None),
            P(),
            P("ctx"),
            P("ctx"),
        ),
        out_specs=(
            P("ctx", "head", None),
            P("ctx", "head", None),
            P("ctx", "head", None),
            P("ctx", "head", None),
            P("ctx", "head", None),
            P("ctx", "head", None),
            P(),
        ),
        check_vma=False,
    )
```

profile of v0, /device:TPU:1, one launch (start us, length us, event | category | flops | bytes accessed | tf_op | source)
XLA Modules:
  0.0 1014.4 jit_solution(6834789810668962888)
XLA Ops:
  10.8 10.2 %collective-permute-start.7 = (bf16[128,128]{1,0:T(8,128)(2,1)S(1)}, bf16[128,128]{1,0:T(8,128)(2,1)S(1)}, u32[]{:S(2)}, u32[]{:S(2)}) collective-permute-start(bf16[128,128]{1,0:T(8,128)(2,1)S(1)} %pad_maximum_fusion.8), channel_id=1, source_target_pairs={{0,28},{4,32},{8,36},{12,40},{16,44},{20,48},{24,52},{28,56},{32,6... | collective-permute-start | bytes 98312 | tf_op jit(solution)/shard_map/ppermute | solution.py:16
  21.0 6.3 collective-permute-start.8
  27.3 5.2 collective-permute-start.9
  32.5 3.1 collective-permute-start.10
  35.6 5.1 collective-permute-start
  43.2 72.9 %all-gather.1 = bf16[128,2,128]{2,1,0:T(2,128)(2,1)S(1)} all-gather(bf16[1,2,128]{2,1,0:T(2,128)(2,1)S(1)} %maximum_bitcast_fusion), channel_id=1, replica_groups=mesh['ctx'=128,'head'=4] {'ctx'}, dimensions={0}, use_global_device_ids=true | all-gather | bytes 66048 | tf_op jit(solution)/shard_map/all_gather | solution.py:99
  117.5 81.3 %all-gather = bf16[256,1,128]{2,1,0:T(2,128)(2,1)S(1)} all-gather(bf16[2,1,128]{2,1,0:T(2,128)(2,1)S(1)} %copy.30), channel_id=2, replica_groups=mesh['ctx'=128,'head'=4] {'ctx'}, dimensions={0}, use_global_device_ids=true | all-gather | bytes 66048 | tf_op jit(solution)/shard_map/all_gather | solution.py:100
  201.2 1.3 dynamic-slice
  203.2 3.9 collective-permute-start.1
  207.4 7.1 collective-permute-start.2
  214.8 4.9 collective-permute-start.3
  220.1 8.2 collective-permute-start.4
  228.6 3.1 collective-permute-start.5
  231.9 5.7 collective-permute-start.6
  238.5 5.8 collective-permute-start.11
  244.3 4.6 stack.93
  248.8 12.0 %while.48 = (s32[]{:T(128)}, s32[1]{0:T(128)}, pred[1,8]{1,0:T(4,128)(4,1)S(1)}, s32[1]{0:T(128)}, s32[]{:T(128)}, /*index=5*/s32[8,1]{0,1:T(1,128)S(1)}, s32[]{:T(128)}, s32[1]{0:T(128)}, s32[1]{0:T(128)}, s32[]{:T(128)}) while((s32[]{:T(128)}, s32[1]{0:T(128)}, pred[1,8]{1,0:T(4,128)(4,1)S(1)}, s32[1]{0:T(128)}, s32[]{:T(128)}, ...), condition=%wide.region_4.0_spmd.clone, body=%wide.region_2.4_spmd.clone.sunk | while | flops 71 | bytes 240 | solution.py:130
  260.9 5.7 collective-permute-start.12
  266.6 3.7 collective-permute-start.13
  270.3 4.0 collective-permute-start.14
  274.3 5.8 collective-permute-start.15
  280.1 5.7 collective-permute-start.16
  285.8 1.9 collective-permute-start.17
  287.8 9.6 collective-permute-start.18
  297.5 18.9 %while.49 = (s32[]{:T(128)}, f32[130,8]{1,0:T(8,128)S(1)}, s32[5]{0:T(128)S(1)}, s32[130]{0:T(256)S(1)}, pred[130,8]{1,0:T(8,128)(4,1)S(1)}, /*index=5*/bf16[5,2...) while((s32[]{:T(128)}, f32[130,8]{1,0:T(8,128)S(1)}, ...), condition=%wide.region_9.10_spmd.clone, body=%wide.region_6.0_spmd.clone.sunk | while | flops 69731088 | bytes 506427 | solution.py:199
  316.4 2.0 collective-permute-start.19
  318.4 2.9 collective-permute-start.20
  323.1 35.6 %while.50 = (s32[]{:T(128)}, f32[1040,128]{1,0:T(8,128)S(1)}, f32[5,256,128]{2,1,0:T(8,128)}, f32[5,256,128]{2,1,0:T(8,128)}, s32[5]{0:T(128)S(1)}, /*index=5*/s...) while((s32[]{:T(128)}, f32[1040,128]{1,0:T(8,128)S(1)}, ...), condition=%wide.wide.region_13.14_spmd.clone, body=%wide.wide.region_11.13_spmd.clone.sunk | while | flops 343723776 | bytes 7544631 | solution.py:227
  358.7 1.6 slice_bitcast_fusion.1
  363.4 1.9 collective-permute-start.21
  365.4 1.3 collective-permute-start.22
  366.7 1.3 collective-permute-start.23
  368.0 1.3 collective-permute-start.24
  369.3 1.3 collective-permute-start.25
  372.8 485.7 %all-reduce.9 = bf16[256,128]{1,0:T(8,128)(2,1)S(1)} all-reduce(f32[256,128]{1,0:T(8,128)S(1)} %slice_bitcast_fusion), channel_id=4, replica_groups=mesh['ctx'=128,'head'=4] {'ctx'}, use_global_device_ids=true, to_apply=%region_18.19.clone | all-reduce | flops 32768 | bytes 196608
  859.8 1.3 collective-permute-start.27
  863.1 7.5 collective-permute-start.28
  870.7 1.3 collective-permute-start.29
  872.0 1.3 collective-permute-start.30
  873.3 1.3 collective-permute-start.31
  874.6 1.3 collective-permute-start.32
  876.5 1.3 collective-permute-start.33
  877.8 1.3 collective-permute-start.34
  879.1 1.7 collective-permute-done.31
  880.8 4.1 collective-permute-done.32
  884.9 2.7 collective-permute-done.33
  887.6 5.2 collective-permute-done.34
  895.2 111.2 %all-reduce.4 = (f32[128]{0:T(128)S(1)}, f32[128]{0:T(128)S(1)}) all-reduce(f32[128]{0:T(128)S(1)} %add.378, f32[128]{0:T(128)S(1)} %get-tuple-element.496), channel_id=1, replica_groups=mesh['ctx'=128,'head'=4] {'ctx','head'}, use_global_device_ids=true, to_apply=%region_23.24 | all-reduce | flops 256 | bytes 2048 | tf_op jit(solution)/shard_map/psum | solution.py:257
  (279 shorter events, 85.5 us)
Async XLA Ops:
  7.2 110.0 %copy-start.11 = (bf16[2,1,1024]{2,0,1:T(2,128)(2,1)S(1)}, bf16[2,1,1024]{2,0,1:T(2,128)(2,1)}, u32[]{:S(2)}) copy-start(bf16[2,1,1024]{2,0,1:T(2,128)(2,1)} %param.24) | copy-start | bytes 12292
  7.2 110.3 %copy-start.12 = (bf16[2,1,128]{2,0,1:T(2,128)(2,1)S(1)}, bf16[2,1,128]{2,0,1:T(2,128)(2,1)}, u32[]{:S(2)}) copy-start(bf16[2,1,128]{2,0,1:T(2,128)(2,1)} %param.26) | copy-start | bytes 1540
  7.2 191.6 %copy-start.4 = (bf16[128,1,1024]{2,0,1:T(8,128)(2,1)S(1)}, bf16[128,1,1024]{2,0,1:T(8,128)(2,1)}, u32[]{:S(2)}) copy-start(bf16[128,1,1024]{2,0,1:T(8,128)(2,1)} %param.23) | copy-start | bytes 786436
  7.2 191.6 %copy-start.9 = (bf16[2,1,1024]{2,0,1:T(2,128)(2,1)S(1)}, bf16[2,1,1024]{2,0,1:T(2,128)(2,1)}, u32[]{:S(2)}) copy-start(bf16[2,1,1024]{2,0,1:T(2,128)(2,1)} %param.28) | copy-start | bytes 12292
  7.2 887.0 %all-reduce.8.cloned.1.call-start = ((), (), s32[]{:S(2)}) async-start(), calls=%async_computation | async-start | bytes 262144
  10.8 250.1 %collective-permute-start.7 = (bf16[128,128]{1,0:T(8,128)(2,1)S(1)}, bf16[128,128]{1,0:T(8,128)(2,1)S(1)}, u32[]{:S(2)}, u32[]{:S(2)}) collective-permute-start(bf16[128,128]{1,0:T(8,128)(2,1)S(1)} %pad_maximum_fusion.8), channel_id=1, source_target_pairs={{0,28},{4,32},{8,36},{12,40},{16,44},{20,48},{24,52},{28,56},{32,6... | collective-permute-start | bytes 98312 | tf_op jit(solution)/shard_map/ppermute | solution.py:16
  21.0 245.6 %collective-permute-start.8 = (bf16[128,128]{1,0:T(8,128)(2,1)S(1)}, bf16[128,128]{1,0:T(8,128)(2,1)S(1)}, u32[]{:S(2)}, u32[]{:S(2)}) collective-permute-start(bf16[128,128]{1,0:T(8,128)(2,1)S(1)} %pad_maximum_fusion.8), channel_id=1, source_target_pairs={{0,24},{4,28},{8,32},{12,36},{16,40},{20,44},{24,48},{28,52},{32,5... | collective-permute-start | bytes 98312 | tf_op jit(solution)/shard_map/ppermute | solution.py:16
  27.3 243.0 %collective-permute-start.9 = (bf16[128,128]{1,0:T(8,128)(2,1)S(1)}, bf16[128,128]{1,0:T(8,128)(2,1)S(1)}, u32[]{:S(2)}, u32[]{:S(2)}) collective-permute-start(bf16[128,128]{1,0:T(8,128)(2,1)S(1)} %pad_maximum_fusion.8), channel_id=1, source_target_pairs={{0,20},{4,24},{8,28},{12,32},{16,36},{20,40},{24,44},{28,48},{32,5... | collective-permute-start | bytes 98312 | tf_op jit(solution)/shard_map/ppermute | solution.py:16
  32.5 241.8 %collective-permute-start.10 = (bf16[128,128]{1,0:T(8,128)(2,1)S(1)}, bf16[128,128]{1,0:T(8,128)(2,1)S(1)}, u32[]{:S(2)}, u32[]{:S(2)}) collective-permute-start(bf16[128,128]{1,0:T(8,128)(2,1)S(1)} %pad_maximum_fusion.8), channel_id=1, source_target_pairs={{0,16},{4,20},{8,24},{12,28},{16,32},{20,36},{24,40},{28,44},{32,4... | collective-permute-start | bytes 98312 | tf_op jit(solution)/shard_map/ppermute | solution.py:16
  35.6 167.6 %collective-permute-start = (s32[1]{0:T(128)}, s32[1]{0:T(128)}, u32[]{:S(2)}, u32[]{:S(2)}) collective-permute-start(s32[1]{0:T(128)} %param.30), channel_id=1, source_target_pairs={{0,28},{4,32},{8,36},{12,40},{16,44},{20,48},{24,52},{28,56},{32,6... | collective-permute-start | bytes 20 | tf_op jit(solution)/shard_map/ppermute | solution.py:16
  117.2 81.8 %copy-start.3 = (bf16[128,1,1024]{2,0,1:T(8,128)(2,1)S(1)}, bf16[128,1,1024]{2,0,1:T(8,128)(2,1)}, u32[]{:S(2)}) copy-start(bf16[128,1,1024]{2,0,1:T(8,128)(2,1)} %param.22) | copy-start | bytes 786436
  117.2 81.8 %copy-start.10 = (bf16[2,1,1024]{2,0,1:T(2,128)(2,1)S(1)}, bf16[2,1,1024]{2,0,1:T(2,128)(2,1)}, u32[]{:S(2)}) copy-start(bf16[2,1,1024]{2,0,1:T(2,128)(2,1)} %param.27) | copy-start | bytes 12292
  200.7 69.6 %copy-start.7 = (bf16[128,1,128]{2,0,1:T(8,128)(2,1)S(1)}, bf16[128,1,128]{2,0,1:T(8,128)(2,1)}, u32[]{:S(2)}) copy-start(bf16[128,1,128]{2,0,1:T(8,128)(2,1)} %param.21) | copy-start | bytes 98308
  200.9 96.6 %copy-start.5 = (s32[130]{0:T(256)S(1)}, s32[130]{0:T(256)}, u32[]{:S(2)}) copy-start(s32[130]{0:T(256)} %constant.212.clone.2) | copy-start | bytes 1564
  200.9 96.6 %copy-start.6 = (s32[130]{0:T(256)S(1)}, s32[130]{0:T(256)}, u32[]{:S(2)}) copy-start(s32[130]{0:T(256)} %constant.214.clone.2) | copy-start | bytes 1564
  203.2 4.2 collective-permute-start.1
  207.4 7.4 collective-permute-start.2
  214.8 5.3 collective-permute-start.3
  220.1 8.5 collective-permute-start.4
  228.6 3.4 collective-permute-start.5
  231.9 6.5 collective-permute-start.6
  238.5 41.7 %collective-permute-start.11 = (bf16[128,128]{1,0:T(8,128)(2,1)S(1)}, bf16[128,128]{1,0:T(8,128)(2,1)S(1)}, u32[]{:S(2)}, u32[]{:S(2)}) collective-permute-start(bf16[128,128]{1,0:T(8,128)(2,1)S(1)} %pad_maximum_fusion.8), channel_id=1, source_target_pairs={{0,12},{4,16},{8,20},{12,24},{16,28},{20,32},{24,36},{28,40},{32,4... | collective-permute-start | bytes 98312 | tf_op jit(solution)/shard_map/ppermute | solution.py:16
  260.9 24.9 %collective-permute-start.12 = (bf16[128,128]{1,0:T(8,128)(2,1)S(1)}, bf16[128,128]{1,0:T(8,128)(2,1)S(1)}, u32[]{:S(2)}, u32[]{:S(2)}) collective-permute-start(bf16[128,128]{1,0:T(8,128)(2,1)S(1)} %pad_maximum_fusion.8), channel_id=1, source_target_pairs={{0,8},{4,12},{8,16},{12,20},{16,24},{20,28},{24,32},{28,36},{32,40... | collective-permute-start | bytes 98312 | tf_op jit(solution)/shard_map/ppermute | solution.py:16
  266.6 21.2 %collective-permute-start.13 = (bf16[128,128]{1,0:T(8,128)(2,1)S(1)}, bf16[128,128]{1,0:T(8,128)(2,1)S(1)}, u32[]{:S(2)}, u32[]{:S(2)}) collective-permute-start(bf16[128,128]{1,0:T(8,128)(2,1)S(1)} %pad_maximum_fusion.8), channel_id=1, source_target_pairs={{0,4},{4,8},{8,12},{12,16},{16,20},{20,24},{24,28},{28,32},{32,36}... | collective-permute-start | bytes 98312 | tf_op jit(solution)/shard_map/ppermute | solution.py:16
  270.3 46.1 %collective-permute-start.14 = (bf16[128,128]{1,0:T(8,128)(2,1)S(1)}, bf16[128,128]{1,0:T(8,128)(2,1)S(1)}, u32[]{:S(2)}, u32[]{:S(2)}) collective-permute-start(bf16[128,128]{1,0:T(8,128)(2,1)S(1)} %bitcast.351), channel_id=1, source_target_pairs={{0,28},{4,32},{8,36},{12,40},{16,44},{20,48},{24,52},{28,56},{32,6... | collective-permute-start | bytes 98312 | tf_op jit(solution)/shard_map/ppermute | solution.py:16
  274.3 44.1 %collective-permute-start.15 = (bf16[128,128]{1,0:T(8,128)(2,1)S(1)}, bf16[128,128]{1,0:T(8,128)(2,1)S(1)}, u32[]{:S(2)}, u32[]{:S(2)}) collective-permute-start(bf16[128,128]{1,0:T(8,128)(2,1)S(1)} %bitcast.352), channel_id=1, source_target_pairs={{0,24},{4,28},{8,32},{12,36},{16,40},{20,44},{24,48},{28,52},{32,5... | collective-permute-start | bytes 98312 | tf_op jit(solution)/shard_map/ppermute | solution.py:16
  280.1 41.2 %collective-permute-start.16 = (bf16[128,128]{1,0:T(8,128)(2,1)S(1)}, bf16[128,128]{1,0:T(8,128)(2,1)S(1)}, u32[]{:S(2)}, u32[]{:S(2)}) collective-permute-start(bf16[128,128]{1,0:T(8,128)(2,1)S(1)} %bitcast.353), channel_id=1, source_target_pairs={{0,20},{4,24},{8,28},{12,32},{16,36},{20,40},{24,44},{28,48},{32,5... | collective-permute-start | bytes 98312 | tf_op jit(solution)/shard_map/ppermute | solution.py:16
  285.8 35.5 %collective-permute-start.17 = (bf16[128,128]{1,0:T(8,128)(2,1)S(1)}, bf16[128,128]{1,0:T(8,128)(2,1)S(1)}, u32[]{:S(2)}, u32[]{:S(2)}) collective-permute-start(bf16[128,128]{1,0:T(8,128)(2,1)S(1)} %bitcast.354), channel_id=1, source_target_pairs={{0,16},{4,20},{8,24},{12,28},{16,32},{20,36},{24,40},{28,44},{32,4... | collective-permute-start | bytes 98312 | tf_op jit(solution)/shard_map/ppermute | solution.py:16
  287.8 33.6 %collective-permute-start.18 = (bf16[128,128]{1,0:T(8,128)(2,1)S(1)}, bf16[128,128]{1,0:T(8,128)(2,1)S(1)}, u32[]{:S(2)}, u32[]{:S(2)}) collective-permute-start(bf16[128,128]{1,0:T(8,128)(2,1)S(1)} %bitcast.355), channel_id=1, source_target_pairs={{0,12},{4,16},{8,20},{12,24},{16,28},{20,32},{24,36},{28,40},{32,4... | collective-permute-start | bytes 98312 | tf_op jit(solution)/shard_map/ppermute | solution.py:16
  316.4 5.0 collective-permute-start.19
  318.4 3.9 collective-permute-start.20
  321.5 1.6 copy-start.2
  363.4 495.1 %collective-permute-start.21 = (bf16[128,128]{1,0:T(8,128)(2,1)S(1)}, bf16[128,128]{1,0:T(8,128)(2,1)S(1)}, u32[]{:S(2)}, u32[]{:S(2)}) collective-permute-start(bf16[128,128]{1,0:T(8,128)(2,1)S(1)} %get-tuple-element.575), channel_id=1, source_target_pairs={{4,0},{8,4},{12,8},{16,12},{20,16},{24,20},{28,24},{32,28},{36,32}... | collective-permute-start | bytes 98312 | tf_op jit(solution)/shard_map/ppermute | solution.py:16
  365.4 494.4 %collective-permute-start.22 = (bf16[128,128]{1,0:T(8,128)(2,1)S(1)}, bf16[128,128]{1,0:T(8,128)(2,1)S(1)}, u32[]{:S(2)}, u32[]{:S(2)}) collective-permute-start(bf16[128,128]{1,0:T(8,128)(2,1)S(1)} %get-tuple-element.581), channel_id=1, source_target_pairs={{8,0},{12,4},{16,8},{20,12},{24,16},{28,20},{32,24},{36,28},{40,32... | collective-permute-start | bytes 98312 | tf_op jit(solution)/shard_map/ppermute | solution.py:16
  366.7 496.4 %collective-permute-start.23 = (bf16[128,128]{1,0:T(8,128)(2,1)S(1)}, bf16[128,128]{1,0:T(8,128)(2,1)S(1)}, u32[]{:S(2)}, u32[]{:S(2)}) collective-permute-start(bf16[128,128]{1,0:T(8,128)(2,1)S(1)} %get-tuple-element.580), channel_id=1, source_target_pairs={{12,0},{16,4},{20,8},{24,12},{28,16},{32,20},{36,24},{40,28},{44,3... | collective-permute-start | bytes 98312 | tf_op jit(solution)/shard_map/ppermute | solution.py:16
  368.0 502.7 %collective-permute-start.24 = (bf16[128,128]{1,0:T(8,128)(2,1)S(1)}, bf16[128,128]{1,0:T(8,128)(2,1)S(1)}, u32[]{:S(2)}, u32[]{:S(2)}) collective-permute-start(bf16[128,128]{1,0:T(8,128)(2,1)S(1)} %get-tuple-element.579), channel_id=1, source_target_pairs={{16,0},{20,4},{24,8},{28,12},{32,16},{36,20},{40,24},{44,28},{48,3... | collective-permute-start | bytes 98312 | tf_op jit(solution)/shard_map/ppermute | solution.py:16
  369.3 502.7 %collective-permute-start.25 = (bf16[128,128]{1,0:T(8,128)(2,1)S(1)}, bf16[128,128]{1,0:T(8,128)(2,1)S(1)}, u32[]{:S(2)}, u32[]{:S(2)}) collective-permute-start(bf16[128,128]{1,0:T(8,128)(2,1)S(1)} %get-tuple-element.578), channel_id=1, source_target_pairs={{20,0},{24,4},{28,8},{32,12},{36,16},{40,20},{44,24},{48,28},{52,3... | collective-permute-start | bytes 98312 | tf_op jit(solution)/shard_map/ppermute | solution.py:16
  372.8 503.5 %copy-start = (bf16[128,1,128]{2,0,1:T(8,128)(2,1)S(1)}, bf16[128,1,128]{2,0,1:T(8,128)(2,1)}, u32[]{:S(2)}) copy-start(bf16[128,1,128]{2,0,1:T(8,128)(2,1)} %param.20) | copy-start | bytes 98308
  858.5 14.8 %collective-permute-start.26 = (bf16[128,128]{1,0:T(8,128)(2,1)S(1)}, bf16[128,128]{1,0:T(8,128)(2,1)S(1)}, u32[]{:S(2)}, u32[]{:S(2)}) collective-permute-start(bf16[128,128]{1,0:T(8,128)(2,1)S(1)} %get-tuple-element.577), channel_id=1, source_target_pairs={{24,0},{28,4},{32,8},{36,12},{40,16},{44,20},{48,24},{52,28},{56,3... | collective-permute-start | bytes 98312 | tf_op jit(solution)/shard_map/ppermute | solution.py:16
  859.8 14.8 %collective-permute-start.27 = (bf16[128,128]{1,0:T(8,128)(2,1)S(1)}, bf16[128,128]{1,0:T(8,128)(2,1)S(1)}, u32[]{:S(2)}, u32[]{:S(2)}) collective-permute-start(bf16[128,128]{1,0:T(8,128)(2,1)S(1)} %get-tuple-element.576), channel_id=1, source_target_pairs={{28,0},{32,4},{36,8},{40,12},{44,16},{48,20},{52,24},{56,28},{60,3... | collective-permute-start | bytes 98312 | tf_op jit(solution)/shard_map/ppermute | solution.py:16
  861.7 33.3 %copy-start.8 = (bf16[2,1,128]{2,0,1:T(2,128)(2,1)S(1)}, bf16[2,1,128]{2,0,1:T(2,128)(2,1)}, u32[]{:S(2)}) copy-start(bf16[2,1,128]{2,0,1:T(2,128)(2,1)} %param.25) | copy-start | bytes 1540
  863.1 13.4 %collective-permute-start.28 = (bf16[128,128]{1,0:T(8,128)(2,1)S(1)}, bf16[128,128]{1,0:T(8,128)(2,1)S(1)}, u32[]{:S(2)}, u32[]{:S(2)}) collective-permute-start(bf16[128,128]{1,0:T(8,128)(2,1)S(1)} %get-tuple-element.568), channel_id=1, source_target_pairs={{4,0},{8,4},{12,8},{16,12},{20,16},{24,20},{28,24},{32,28},{36,32}... | collective-permute-start | bytes 98312 | tf_op jit(solution)/shard_map/ppermute | solution.py:16
  870.7 7.1 collective-permute-start.29
  872.0 7.1 collective-permute-start.30
  873.3 7.5 collective-permute-start.31
  874.6 10.3 %collective-permute-start.32 = (bf16[128,128]{1,0:T(8,128)(2,1)S(1)}, bf16[128,128]{1,0:T(8,128)(2,1)S(1)}, u32[]{:S(2)}, u32[]{:S(2)}) collective-permute-start(bf16[128,128]{1,0:T(8,128)(2,1)S(1)} %get-tuple-element.571), channel_id=1, source_target_pairs={{20,0},{24,4},{28,8},{32,12},{36,16},{40,20},{44,24},{48,28},{52,3... | collective-permute-start | bytes 98312 | tf_op jit(solution)/shard_map/ppermute | solution.py:16
  876.5 11.1 %collective-permute-start.33 = (bf16[128,128]{1,0:T(8,128)(2,1)S(1)}, bf16[128,128]{1,0:T(8,128)(2,1)S(1)}, u32[]{:S(2)}, u32[]{:S(2)}) collective-permute-start(bf16[128,128]{1,0:T(8,128)(2,1)S(1)} %get-tuple-element.570), channel_id=1, source_target_pairs={{24,0},{28,4},{32,8},{36,12},{40,16},{44,20},{48,24},{52,28},{56,3... | collective-permute-start | bytes 98312 | tf_op jit(solution)/shard_map/ppermute | solution.py:16
  877.8 15.0 %collective-permute-start.34 = (bf16[128,128]{1,0:T(8,128)(2,1)S(1)}, bf16[128,128]{1,0:T(8,128)(2,1)S(1)}, u32[]{:S(2)}, u32[]{:S(2)}) collective-permute-start(bf16[128,128]{1,0:T(8,128)(2,1)S(1)} %get-tuple-element.569), channel_id=1, source_target_pairs={{28,0},{32,4},{36,8},{40,12},{44,16},{48,20},{52,24},{56,28},{60,3... | collective-permute-start | bytes 98312 | tf_op jit(solution)/shard_map/ppermute | solution.py:16
  (1 other events, 0.9 us)
Sparse Core Ops, SparseCore 0:
  363.5 318.1 all-reduce.7
where the time goes:
time: 1020 us; the launch traced here: 1010 us
  blocking collectives  751 us (74%)
  starting transfers between devices  135 us (13%)
  other arithmetic  43.4 us (4%)
  local copies, waits for them, and re-layouts  22.6 us (2%)
  matrix products  22.5 us (2%)
  waiting for transfers between devices  16.9 us (2%)
  between operations  16.4 us (2%)
    unnamed x1, blocking collectives  486 us
    ppermute x35, starting transfers between devices, shifted(): lax.ppermute(value, axis, [(source, source + steps) for source in range(l...  135 us
    psum x1, blocking collectives, per_device(): sum_q, sum_k = lax.psum((gain_part_q, gain_bk + gain_pk), ('ctx', 'head'))  111 us
    all_gather x1, blocking collectives, per_device(): lax.all_gather(prompt_v[:, 0], 'ctx', axis=0, tiled=True)  81.3 us
    all_gather x1, blocking collectives, per_device(): lax.all_gather(rotated_pk, 'ctx', axis=0, tiled=True)  72.9 us
  transfers between devices with their start and end apart: 36, of which 11 were waited for; matrix products, arithmetic and copies ran while one was open for 4% of the time, Pallas kernels for 0%

commit v1 on v0

--- a/solution.py
+++ b/solution.py
@@ -8,6 +8,13 @@
 PFX = 256
 EPS = 1e-06
 THETA = 1000000.0
+
+
+def close_sizes(u_in, shard_axis):
+    return jnp.concatenate(
+        lax.all_to_all(jnp.stack(lax.axis_size(shard_axis) * [u_in], axis=0), shard_axis, 0, 0),
+        axis=0,
+    )
 
 
 def shifted(value, axis, steps):
@@ -97,7 +104,7 @@
     value_local = branch_v[:, 0]
     prompt_keys, prompt_values = (
         lax.all_gather(rotated_pk, "ctx", axis=0, tiled=True),
-        lax.all_gather(prompt_v[:, 0], "ctx", axis=0, tiled=True),
+        close_sizes(prompt_v[:, 0], "ctx"),
     )
     fetched = [(rotated_bk, value_local, parents)]
     for distance in range(1, reach_back + 1):

time: 1020 us -> 955 us (0.936)
  blocking collectives: 751 us -> 675 us
  starting transfers between devices: 135 us -> 147 us
    all_gather x1 -> x0, blocking collectives: 81.3 us -> none  [per_device(): lax.all_gather(prompt_v[:, 0], 'ctx', axis=0, tiled=True)]
    all_to_all x0 -> x1, starting transfers between devices: none -> 11.6 us  [close_sizes(): lax.all_to_all(jnp.stack(lax.axis_size(shard_axis) * [u_in], axis=0), sha...]
  transfers between devices with their start and end apart: 36 -> 37, of which waited for: 11 -> 11; matrix products, arithmetic and copies ran while one was open for 4% -> 4% of each run, Pallas kernels for 0% -> 0%
where the time goes in v1:
time: 955 us; the launch traced here: 952 us
  blocking collectives  675 us (71%)
  starting transfers between devices  147 us (15%)
  other arithmetic  43.4 us (5%)
  local copies, waits for them, and re-layouts  23.9 us (3%)
  matrix products  22.5 us (2%)
  waiting for transfers between devices  16.9 us (2%)
  between operations  16.4 us (2%)
    unnamed x1, blocking collectives  486 us
    ppermute x35, starting transfers between devices, shifted(): lax.ppermute(value, axis, [(source, source + steps) for source in range(l...  136 us
    psum x1, blocking collectives, per_device(): sum_q, sum_k = lax.psum((gain_part_q, gain_bk + gain_pk), ('ctx', 'head'))  111 us
    all_gather x1, blocking collectives, per_device(): lax.all_gather(rotated_pk, 'ctx', axis=0, tiled=True)  78.1 us
  transfers between devices with their start and end apart: 37, of which 11 were waited for; matrix products, arithmetic and copies ran while one was open for 4% of the time, Pallas kernels for 0%

profile of v1, /device:TPU:1, one launch (start us, length us, event | category | flops | bytes accessed | tf_op | source)
XLA Modules:
  0.0 952.4 jit_solution(14283316539559308929)
XLA Ops:
  10.8 10.2 %collective-permute-start.7 = (bf16[128,128]{1,0:T(8,128)(2,1)S(1)}, bf16[128,128]{1,0:T(8,128)(2,1)S(1)}, u32[]{:S(2)}, u32[]{:S(2)}) collective-permute-start(bf16[128,128]{1,0:T(8,128)(2,1)S(1)} %pad_maximum_fusion.8), channel_id=1, source_target_pairs={{0,28},{4,32},{8,36},{12,40},{16,44},{20,48},{24,52},{28,56},{32,6... | collective-permute-start | bytes 98312 | tf_op jit(solution)/shard_map/ppermute | solution.py:23
  21.0 6.3 collective-permute-start.8
  27.2 5.2 collective-permute-start.9
  32.5 3.1 collective-permute-start.10
  35.6 5.1 collective-permute-start
  40.7 1.3 stack.105
  42.0 11.6 %all-to-all-start = ((bf16[128,2,128]{2,1,0:T(2,128)(2,1)}), bf16[128,2,128]{2,1,0:T(2,128)(2,1)S(1)}, u32[]{:S(2)}, u32[]{:S(2)}) async-start(bf16[128,2,128]{2,1,0:T(2,128)(2,1)} %stack.105), calls=%async_computation | async-start | bytes 131072 | tf_op jit(solution)/shard_map/all_to_all | solution.py:15
  56.1 78.1 %all-gather = bf16[128,2,128]{2,1,0:T(2,128)(2,1)S(1)} all-gather(bf16[1,2,128]{2,1,0:T(2,128)(2,1)S(1)} %maximum_bitcast_fusion), channel_id=1, replica_groups=mesh['ctx'=128,'head'=4] {'ctx'}, dimensions={0}, use_global_device_ids=true | all-gather | bytes 66048 | tf_op jit(solution)/shard_map/all_gather | solution.py:106
  138.0 1.4 dynamic-slice
  140.1 3.4 collective-permute-start.1
  143.8 7.8 collective-permute-start.2
  151.9 5.6 collective-permute-start.3
  157.8 9.3 collective-permute-start.4
  167.3 2.2 collective-permute-start.5
  169.8 6.4 collective-permute-start.6
  177.1 5.8 collective-permute-start.11
  182.9 4.6 stack.96
  187.4 12.0 %while.48 = (s32[]{:T(128)}, s32[1]{0:T(128)}, pred[1,8]{1,0:T(4,128)(4,1)S(1)}, s32[1]{0:T(128)}, s32[]{:T(128)}, /*index=5*/s32[8,1]{0,1:T(1,128)S(1)}, s32[]{:T(128)}, s32[1]{0:T(128)}, s32[1]{0:T(128)}, s32[]{:T(128)}) while((s32[]{:T(128)}, s32[1]{0:T(128)}, pred[1,8]{1,0:T(4,128)(4,1)S(1)}, s32[1]{0:T(128)}, s32[]{:T(128)}, ...), condition=%wide.region_4.0_spmd.clone, body=%wide.region_2.4_spmd.clone.sunk | while | flops 71 | bytes 240 | solution.py:137
  199.5 5.7 collective-permute-start.12
  205.2 3.7 collective-permute-start.13
  208.9 4.0 collective-permute-start.14
  212.9 4.8 collective-permute-start.15
  217.8 3.7 collective-permute-start.16
  221.5 3.9 collective-permute-start.17
  225.5 9.6 %collective-permute-start.18 = (bf16[128,128]{1,0:T(8,128)(2,1)S(1)}, bf16[128,128]{1,0:T(8,128)(2,1)S(1)}, u32[]{:S(2)}, u32[]{:S(2)}) collective-permute-start(bf16[128,128]{1,0:T(8,128)(2,1)S(1)} %bitcast.354), channel_id=1, source_target_pairs={{0,12},{4,16},{8,20},{12,24},{16,28},{20,32},{24,36},{28,40},{32,4... | collective-permute-start | bytes 98312 | tf_op jit(solution)/shard_map/ppermute | solution.py:23
  235.2 18.9 %while.49 = (s32[]{:T(128)}, f32[130,8]{1,0:T(8,128)S(1)}, s32[5]{0:T(128)S(1)}, s32[130]{0:T(256)S(1)}, pred[130,8]{1,0:T(8,128)(4,1)S(1)}, /*index=5*/bf16[5,2...) while((s32[]{:T(128)}, f32[130,8]{1,0:T(8,128)S(1)}, ...), condition=%wide.region_9.10_spmd.clone, body=%wide.region_6.0_spmd.clone.sunk | while | flops 69731088 | bytes 506427 | solution.py:206
  254.1 1.9 collective-permute-start.19
  256.1 2.9 collective-permute-start.20
  260.9 35.5 %while.50 = (s32[]{:T(128)}, f32[1040,128]{1,0:T(8,128)S(1)}, f32[5,256,128]{2,1,0:T(8,128)}, f32[5,256,128]{2,1,0:T(8,128)}, s32[5]{0:T(128)S(1)}, /*index=5*/s...) while((s32[]{:T(128)}, f32[1040,128]{1,0:T(8,128)S(1)}, ...), condition=%wide.wide.region_13.14_spmd.clone, body=%wide.wide.region_11.13_spmd.clone.sunk | while | flops 343723776 | bytes 7544631 | solution.py:234
  296.4 1.6 slice_bitcast_fusion.1
  301.2 1.9 collective-permute-start.21
  303.1 1.3 collective-permute-start.22
  304.4 1.3 collective-permute-start.23
  305.7 1.3 collective-permute-start.24
  307.0 1.5 collective-permute-start.25
  310.7 485.7 %all-reduce.9 = bf16[256,128]{1,0:T(8,128)(2,1)S(1)} all-reduce(f32[256,128]{1,0:T(8,128)S(1)} %slice_bitcast_fusion), channel_id=3, replica_groups=mesh['ctx'=128,'head'=4] {'ctx'}, use_global_device_ids=true, to_apply=%region_18.19.clone | all-reduce | flops 32768 | bytes 196608
  797.7 1.3 collective-permute-start.27
  801.0 7.5 collective-permute-start.28
  808.6 1.3 collective-permute-start.29
  809.9 1.3 collective-permute-start.30
  811.2 1.3 collective-permute-start.31
  812.5 1.3 collective-permute-start.32
  814.4 1.3 collective-permute-start.33
  817.0 1.7 collective-permute-done.31
  818.7 4.1 collective-permute-done.32
  822.8 2.7 collective-permute-done.33
  825.5 5.2 collective-permute-done.34
  833.1 111.3 %all-reduce.4 = (f32[128]{0:T(128)S(1)}, f32[128]{0:T(128)S(1)}) all-reduce(f32[128]{0:T(128)S(1)} %add.378, f32[128]{0:T(128)S(1)} %get-tuple-element.496), channel_id=1, replica_groups=mesh['ctx'=128,'head'=4] {'ctx','head'}, use_global_device_ids=true, to_apply=%region_23.24 | all-reduce | flops 256 | bytes 2048 | tf_op jit(solution)/shard_map/psum | solution.py:264
  (277 shorter events, 86.9 us)
Async XLA Ops:
  7.2 128.1 %copy-start.11 = (bf16[2,1,1024]{2,0,1:T(2,128)(2,1)S(1)}, bf16[2,1,1024]{2,0,1:T(2,128)(2,1)}, u32[]{:S(2)}) copy-start(bf16[2,1,1024]{2,0,1:T(2,128)(2,1)} %param.24) | copy-start | bytes 12292
  7.2 128.4 %copy-start.4 = (bf16[128,1,1024]{2,0,1:T(8,128)(2,1)S(1)}, bf16[128,1,1024]{2,0,1:T(8,128)(2,1)}, u32[]{:S(2)}) copy-start(bf16[128,1,1024]{2,0,1:T(8,128)(2,1)} %param.23) | copy-start | bytes 786436
  7.2 128.4 %copy-start.9 = (bf16[2,1,1024]{2,0,1:T(2,128)(2,1)S(1)}, bf16[2,1,1024]{2,0,1:T(2,128)(2,1)}, u32[]{:S(2)}) copy-start(bf16[2,1,1024]{2,0,1:T(2,128)(2,1)} %param.28) | copy-start | bytes 12292
  10.8 188.7 %collective-permute-start.7 = (bf16[128,128]{1,0:T(8,128)(2,1)S(1)}, bf16[128,128]{1,0:T(8,128)(2,1)S(1)}, u32[]{:S(2)}, u32[]{:S(2)}) collective-permute-start(bf16[128,128]{1,0:T(8,128)(2,1)S(1)} %pad_maximum_fusion.8), channel_id=1, source_target_pairs={{0,28},{4,32},{8,36},{12,40},{16,44},{20,48},{24,52},{28,56},{32,6... | collective-permute-start | bytes 98312 | tf_op jit(solution)/shard_map/ppermute | solution.py:23
  21.0 184.2 %collective-permute-start.8 = (bf16[128,128]{1,0:T(8,128)(2,1)S(1)}, bf16[128,128]{1,0:T(8,128)(2,1)S(1)}, u32[]{:S(2)}, u32[]{:S(2)}) collective-permute-start(bf16[128,128]{1,0:T(8,128)(2,1)S(1)} %pad_maximum_fusion.8), channel_id=1, source_target_pairs={{0,24},{4,28},{8,32},{12,36},{16,40},{20,44},{24,48},{28,52},{32,5... | collective-permute-start | bytes 98312 | tf_op jit(solution)/shard_map/ppermute | solution.py:23
  27.2 181.7 %collective-permute-start.9 = (bf16[128,128]{1,0:T(8,128)(2,1)S(1)}, bf16[128,128]{1,0:T(8,128)(2,1)S(1)}, u32[]{:S(2)}, u32[]{:S(2)}) collective-permute-start(bf16[128,128]{1,0:T(8,128)(2,1)S(1)} %pad_maximum_fusion.8), channel_id=1, source_target_pairs={{0,20},{4,24},{8,28},{12,32},{16,36},{20,40},{24,44},{28,48},{32,5... | collective-permute-start | bytes 98312 | tf_op jit(solution)/shard_map/ppermute | solution.py:23
  32.5 180.5 %collective-permute-start.10 = (bf16[128,128]{1,0:T(8,128)(2,1)S(1)}, bf16[128,128]{1,0:T(8,128)(2,1)S(1)}, u32[]{:S(2)}, u32[]{:S(2)}) collective-permute-start(bf16[128,128]{1,0:T(8,128)(2,1)S(1)} %pad_maximum_fusion.8), channel_id=1, source_target_pairs={{0,16},{4,20},{8,24},{12,28},{16,32},{20,36},{24,40},{28,44},{32,4... | collective-permute-start | bytes 98312 | tf_op jit(solution)/shard_map/ppermute | solution.py:23
  35.6 104.5 %collective-permute-start = (s32[1]{0:T(128)}, s32[1]{0:T(128)}, u32[]{:S(2)}, u32[]{:S(2)}) collective-permute-start(s32[1]{0:T(128)} %param.30), channel_id=1, source_target_pairs={{0,28},{4,32},{8,36},{12,40},{16,44},{20,48},{24,52},{28,56},{32,6... | collective-permute-start | bytes 20 | tf_op jit(solution)/shard_map/ppermute | solution.py:23
  42.0 218.1 %all-to-all-start = ((bf16[128,2,128]{2,1,0:T(2,128)(2,1)}), bf16[128,2,128]{2,1,0:T(2,128)(2,1)S(1)}, u32[]{:S(2)}, u32[]{:S(2)}) async-start(bf16[128,2,128]{2,1,0:T(2,128)(2,1)} %stack.105), calls=%async_computation | async-start | bytes 131072 | tf_op jit(solution)/shard_map/all_to_all | solution.py:15
  53.6 778.5 %all-reduce.8.cloned.1.call-start = ((), (), s32[]{:S(2)}) async-start(), calls=%async_computation.1 | async-start | bytes 262144
  134.3 1.5 copy-start.3
  134.3 1.5 copy-start.10
  137.6 71.4 %copy-start.7 = (bf16[128,1,128]{2,0,1:T(8,128)(2,1)S(1)}, bf16[128,1,128]{2,0,1:T(8,128)(2,1)}, u32[]{:S(2)}) copy-start(bf16[128,1,128]{2,0,1:T(8,128)(2,1)} %param.21) | copy-start | bytes 98308
  137.7 97.5 %copy-start.5 = (s32[130]{0:T(256)S(1)}, s32[130]{0:T(256)}, u32[]{:S(2)}) copy-start(s32[130]{0:T(256)} %constant.212.clone.2) | copy-start | bytes 1564
  137.7 97.5 %copy-start.6 = (s32[130]{0:T(256)S(1)}, s32[130]{0:T(256)}, u32[]{:S(2)}) copy-start(s32[130]{0:T(256)} %constant.214.clone.2) | copy-start | bytes 1564
  140.1 3.7 collective-permute-start.1
  143.8 8.1 collective-permute-start.2
  151.9 5.9 collective-permute-start.3
  157.8 9.5 %collective-permute-start.4 = (s32[1]{0:T(128)}, s32[1]{0:T(128)}, u32[]{:S(2)}, u32[]{:S(2)}) collective-permute-start(s32[1]{0:T(128)} %param.30), channel_id=1, source_target_pairs={{0,12},{4,16},{8,20},{12,24},{16,28},{20,32},{24,36},{28,40},{32,4... | collective-permute-start | bytes 20 | tf_op jit(solution)/shard_map/ppermute | solution.py:23
  167.3 2.5 collective-permute-start.5
  169.8 7.3 collective-permute-start.6
  177.1 40.7 %collective-permute-start.11 = (bf16[128,128]{1,0:T(8,128)(2,1)S(1)}, bf16[128,128]{1,0:T(8,128)(2,1)S(1)}, u32[]{:S(2)}, u32[]{:S(2)}) collective-permute-start(bf16[128,128]{1,0:T(8,128)(2,1)S(1)} %pad_maximum_fusion.8), channel_id=1, source_target_pairs={{0,12},{4,16},{8,20},{12,24},{16,28},{20,32},{24,36},{28,40},{32,4... | collective-permute-start | bytes 98312 | tf_op jit(solution)/shard_map/ppermute | solution.py:23
  199.5 22.0 %collective-permute-start.12 = (bf16[128,128]{1,0:T(8,128)(2,1)S(1)}, bf16[128,128]{1,0:T(8,128)(2,1)S(1)}, u32[]{:S(2)}, u32[]{:S(2)}) collective-permute-start(bf16[128,128]{1,0:T(8,128)(2,1)S(1)} %pad_maximum_fusion.8), channel_id=1, source_target_pairs={{0,8},{4,12},{8,16},{12,20},{16,24},{20,28},{24,32},{28,36},{32,40... | collective-permute-start | bytes 98312 | tf_op jit(solution)/shard_map/ppermute | solution.py:23
  205.2 20.3 %collective-permute-start.13 = (bf16[128,128]{1,0:T(8,128)(2,1)S(1)}, bf16[128,128]{1,0:T(8,128)(2,1)S(1)}, u32[]{:S(2)}, u32[]{:S(2)}) collective-permute-start(bf16[128,128]{1,0:T(8,128)(2,1)S(1)} %pad_maximum_fusion.8), channel_id=1, source_target_pairs={{0,4},{4,8},{8,12},{12,16},{16,20},{20,24},{24,28},{28,32},{32,36}... | collective-permute-start | bytes 98312 | tf_op jit(solution)/shard_map/ppermute | solution.py:23
  208.9 45.2 %collective-permute-start.14 = (bf16[128,128]{1,0:T(8,128)(2,1)S(1)}, bf16[128,128]{1,0:T(8,128)(2,1)S(1)}, u32[]{:S(2)}, u32[]{:S(2)}) collective-permute-start(bf16[128,128]{1,0:T(8,128)(2,1)S(1)} %bitcast.350), channel_id=1, source_target_pairs={{0,28},{4,32},{8,36},{12,40},{16,44},{20,48},{24,52},{28,56},{32,6... | collective-permute-start | bytes 98312 | tf_op jit(solution)/shard_map/ppermute | solution.py:23
  212.9 43.1 %collective-permute-start.15 = (bf16[128,128]{1,0:T(8,128)(2,1)S(1)}, bf16[128,128]{1,0:T(8,128)(2,1)S(1)}, u32[]{:S(2)}, u32[]{:S(2)}) collective-permute-start(bf16[128,128]{1,0:T(8,128)(2,1)S(1)} %bitcast.351), channel_id=1, source_target_pairs={{0,24},{4,28},{8,32},{12,36},{16,40},{20,44},{24,48},{28,52},{32,5... | collective-permute-start | bytes 98312 | tf_op jit(solution)/shard_map/ppermute | solution.py:23
  217.8 41.2 %collective-permute-start.16 = (bf16[128,128]{1,0:T(8,128)(2,1)S(1)}, bf16[128,128]{1,0:T(8,128)(2,1)S(1)}, u32[]{:S(2)}, u32[]{:S(2)}) collective-permute-start(bf16[128,128]{1,0:T(8,128)(2,1)S(1)} %bitcast.352), channel_id=1, source_target_pairs={{0,20},{4,24},{8,28},{12,32},{16,36},{20,40},{24,44},{28,48},{32,5... | collective-permute-start | bytes 98312 | tf_op jit(solution)/shard_map/ppermute | solution.py:23
  221.5 37.5 %collective-permute-start.17 = (bf16[128,128]{1,0:T(8,128)(2,1)S(1)}, bf16[128,128]{1,0:T(8,128)(2,1)S(1)}, u32[]{:S(2)}, u32[]{:S(2)}) collective-permute-start(bf16[128,128]{1,0:T(8,128)(2,1)S(1)} %bitcast.353), channel_id=1, source_target_pairs={{0,16},{4,20},{8,24},{12,28},{16,32},{20,36},{24,40},{28,44},{32,4... | collective-permute-start | bytes 98312 | tf_op jit(solution)/shard_map/ppermute | solution.py:23
  225.5 33.6 %collective-permute-start.18 = (bf16[128,128]{1,0:T(8,128)(2,1)S(1)}, bf16[128,128]{1,0:T(8,128)(2,1)S(1)}, u32[]{:S(2)}, u32[]{:S(2)}) collective-permute-start(bf16[128,128]{1,0:T(8,128)(2,1)S(1)} %bitcast.354), channel_id=1, source_target_pairs={{0,12},{4,16},{8,20},{12,24},{16,28},{20,32},{24,36},{28,40},{32,4... | collective-permute-start | bytes 98312 | tf_op jit(solution)/shard_map/ppermute | solution.py:23
  254.1 4.9 collective-permute-start.19
  256.1 3.9 collective-permute-start.20
  301.2 495.3 %collective-permute-start.21 = (bf16[128,128]{1,0:T(8,128)(2,1)S(1)}, bf16[128,128]{1,0:T(8,128)(2,1)S(1)}, u32[]{:S(2)}, u32[]{:S(2)}) collective-permute-start(bf16[128,128]{1,0:T(8,128)(2,1)S(1)} %get-tuple-element.575), channel_id=1, source_target_pairs={{4,0},{8,4},{12,8},{16,12},{20,16},{24,20},{28,24},{32,28},{36,32}... | collective-permute-start | bytes 98312 | tf_op jit(solution)/shard_map/ppermute | solution.py:23
  303.1 494.7 %collective-permute-start.22 = (bf16[128,128]{1,0:T(8,128)(2,1)S(1)}, bf16[128,128]{1,0:T(8,128)(2,1)S(1)}, u32[]{:S(2)}, u32[]{:S(2)}) collective-permute-start(bf16[128,128]{1,0:T(8,128)(2,1)S(1)} %get-tuple-element.581), channel_id=1, source_target_pairs={{8,0},{12,4},{16,8},{20,12},{24,16},{28,20},{32,24},{36,28},{40,32... | collective-permute-start | bytes 98312 | tf_op jit(solution)/shard_map/ppermute | solution.py:23
  304.4 496.6 %collective-permute-start.23 = (bf16[128,128]{1,0:T(8,128)(2,1)S(1)}, bf16[128,128]{1,0:T(8,128)(2,1)S(1)}, u32[]{:S(2)}, u32[]{:S(2)}) collective-permute-start(bf16[128,128]{1,0:T(8,128)(2,1)S(1)} %get-tuple-element.580), channel_id=1, source_target_pairs={{12,0},{16,4},{20,8},{24,12},{28,16},{32,20},{36,24},{40,28},{44,3... | collective-permute-start | bytes 98312 | tf_op jit(solution)/shard_map/ppermute | solution.py:23
  305.7 502.9 %collective-permute-start.24 = (bf16[128,128]{1,0:T(8,128)(2,1)S(1)}, bf16[128,128]{1,0:T(8,128)(2,1)S(1)}, u32[]{:S(2)}, u32[]{:S(2)}) collective-permute-start(bf16[128,128]{1,0:T(8,128)(2,1)S(1)} %get-tuple-element.579), channel_id=1, source_target_pairs={{16,0},{20,4},{24,8},{28,12},{32,16},{36,20},{40,24},{44,28},{48,3... | collective-permute-start | bytes 98312 | tf_op jit(solution)/shard_map/ppermute | solution.py:23
  307.0 502.9 %collective-permute-start.25 = (bf16[128,128]{1,0:T(8,128)(2,1)S(1)}, bf16[128,128]{1,0:T(8,128)(2,1)S(1)}, u32[]{:S(2)}, u32[]{:S(2)}) collective-permute-start(bf16[128,128]{1,0:T(8,128)(2,1)S(1)} %get-tuple-element.578), channel_id=1, source_target_pairs={{20,0},{24,4},{28,8},{32,12},{36,16},{40,20},{44,24},{48,28},{52,3... | collective-permute-start | bytes 98312 | tf_op jit(solution)/shard_map/ppermute | solution.py:23
  308.5 0.9 copy-start.1
  310.7 503.5 %copy-start = (bf16[128,1,128]{2,0,1:T(8,128)(2,1)S(1)}, bf16[128,1,128]{2,0,1:T(8,128)(2,1)}, u32[]{:S(2)}) copy-start(bf16[128,1,128]{2,0,1:T(8,128)(2,1)} %param.20) | copy-start | bytes 98308
  796.4 14.8 %collective-permute-start.26 = (bf16[128,128]{1,0:T(8,128)(2,1)S(1)}, bf16[128,128]{1,0:T(8,128)(2,1)S(1)}, u32[]{:S(2)}, u32[]{:S(2)}) collective-permute-start(bf16[128,128]{1,0:T(8,128)(2,1)S(1)} %get-tuple-element.577), channel_id=1, source_target_pairs={{24,0},{28,4},{32,8},{36,12},{40,16},{44,20},{48,24},{52,28},{56,3... | collective-permute-start | bytes 98312 | tf_op jit(solution)/shard_map/ppermute | solution.py:23
  797.7 14.8 %collective-permute-start.27 = (bf16[128,128]{1,0:T(8,128)(2,1)S(1)}, bf16[128,128]{1,0:T(8,128)(2,1)S(1)}, u32[]{:S(2)}, u32[]{:S(2)}) collective-permute-start(bf16[128,128]{1,0:T(8,128)(2,1)S(1)} %get-tuple-element.576), channel_id=1, source_target_pairs={{28,0},{32,4},{36,8},{40,12},{44,16},{48,20},{52,24},{56,28},{60,3... | collective-permute-start | bytes 98312 | tf_op jit(solution)/shard_map/ppermute | solution.py:23
  799.6 33.3 %copy-start.8 = (bf16[2,1,128]{2,0,1:T(2,128)(2,1)S(1)}, bf16[2,1,128]{2,0,1:T(2,128)(2,1)}, u32[]{:S(2)}) copy-start(bf16[2,1,128]{2,0,1:T(2,128)(2,1)} %param.25) | copy-start | bytes 1540
  801.0 13.4 %collective-permute-start.28 = (bf16[128,128]{1,0:T(8,128)(2,1)S(1)}, bf16[128,128]{1,0:T(8,128)(2,1)S(1)}, u32[]{:S(2)}, u32[]{:S(2)}) collective-permute-start(bf16[128,128]{1,0:T(8,128)(2,1)S(1)} %get-tuple-element.568), channel_id=1, source_target_pairs={{4,0},{8,4},{12,8},{16,12},{20,16},{24,20},{28,24},{32,28},{36,32}... | collective-permute-start | bytes 98312 | tf_op jit(solution)/shard_map/ppermute | solution.py:23
  808.6 7.1 collective-permute-start.29
  809.9 7.1 collective-permute-start.30
  811.2 7.5 collective-permute-start.31
  812.5 10.3 %collective-permute-start.32 = (bf16[128,128]{1,0:T(8,128)(2,1)S(1)}, bf16[128,128]{1,0:T(8,128)(2,1)S(1)}, u32[]{:S(2)}, u32[]{:S(2)}) collective-permute-start(bf16[128,128]{1,0:T(8,128)(2,1)S(1)} %get-tuple-element.571), channel_id=1, source_target_pairs={{20,0},{24,4},{28,8},{32,12},{36,16},{40,20},{44,24},{48,28},{52,3... | collective-permute-start | bytes 98312 | tf_op jit(solution)/shard_map/ppermute | solution.py:23
  814.4 11.1 %collective-permute-start.33 = (bf16[128,128]{1,0:T(8,128)(2,1)S(1)}, bf16[128,128]{1,0:T(8,128)(2,1)S(1)}, u32[]{:S(2)}, u32[]{:S(2)}) collective-permute-start(bf16[128,128]{1,0:T(8,128)(2,1)S(1)} %get-tuple-element.570), channel_id=1, source_target_pairs={{24,0},{28,4},{32,8},{36,12},{40,16},{44,20},{48,24},{52,28},{56,3... | collective-permute-start | bytes 98312 | tf_op jit(solution)/shard_map/ppermute | solution.py:23
  815.7 15.0 %collective-permute-start.34 = (bf16[128,128]{1,0:T(8,128)(2,1)S(1)}, bf16[128,128]{1,0:T(8,128)(2,1)S(1)}, u32[]{:S(2)}, u32[]{:S(2)}) collective-permute-start(bf16[128,128]{1,0:T(8,128)(2,1)S(1)} %get-tuple-element.569), channel_id=1, source_target_pairs={{28,0},{32,4},{36,8},{40,12},{44,16},{48,20},{52,24},{56,28},{60,3... | collective-permute-start | bytes 98312 | tf_op jit(solution)/shard_map/ppermute | solution.py:23
  (1 other events, 0.9 us)
Sparse Core Ops, SparseCore 0:
  301.2 316.7 all-reduce.7
